TPU v7x, 32 devices: a whole 2x2x4 slice. The times are simulated.
32 devices in a mesh: fsdp: 8 (over y, x, core), group: 4 (over z).
Axes of the slice: x: 2, y: 2, z: 4, core: 2. Of those that a mesh axis runs over, the one named last changes fastest.
Arguments:
- gradient: bfloat16 [4, 512, 4096], P('group', 'fsdp'), may hold values from -4000 to 4000
- first_moment: bfloat16 [4, 4096, 512], P('group', 'fsdp'), may hold values from -3 to 3
- second_moment: bfloat16 [4, 4096, 512], P('group', 'fsdp'), may hold values from 0.29882812 to 3
- basis_store: bfloat16 [4, 4608, 256], P('group', 'fsdp'), may hold values from -1 to 2
- step_number: int32 [1], replicated, may hold values from 1 to 99999
- matrix_ids: int32 [4], P('group'), may hold values from 0 to 3, each once
Outputs:
- update: bfloat16 [4, 512, 4096], P('group', 'fsdp')
- new_first: bfloat16 [4, 4096, 512], P('group', 'fsdp')
- new_second: bfloat16 [4, 4096, 512], P('group', 'fsdp')
Inputs may be any that keep to these rules, and one draw needn't show every extreme that they name: `matrix_ids`: each matrix index once.
All inputs are finite; a program needn't handle non-finite values.
Results may differ from a plain program's by a relative error of at most 0.0004.
Values may be sent and summed in bfloat16 or wider, within the bound.
A program may use at most 64 MiB of HBM per device.

v0:
```python
import math

import jax
import jax.numpy as jnp
from jax import lax
from jax.sharding import PartitionSpec as P

BLOCK = 256


BETA_ONE = 0.95
BETA_TWO = 0.95
ADAM_EPS = 1e-08
HIGHEST = lax.Precision.HIGHEST


def clip_of(local_squares, entries):
    total = lax.psum(local_squares, ("fsdp", "group"))
    return jnp.float32(math.sqrt(entries)) / (jnp.sqrt(total) + 1e-06)


def local(gradient, first_moment, second_moment, basis_store, step_number, matrix_ids):
    fsdp_count = lax.axis_size("fsdp")
    group_count = lax.axis_size("group")
    row_count = gradient.shape[1]
    col_count = gradient.shape[2]
    all_rows = row_count * fsdp_count
    col_share = col_count // fsdp_count
    left_blocks = all_rows // BLOCK
    right_blocks = col_count // BLOCK
    entries = all_rows * col_count * group_count
    grad_local = gradient[0].astype(jnp.float32)
    local_squares = jnp.sum(grad_local * grad_local)
    gathered = lax.all_gather(basis_store[0], "fsdp", axis=0, tiled=True)
    owner_rows = basis_store.shape[1]
    owner = (step_number[0] + matrix_ids[0]) % fsdp_count
    ordered_half = jnp.roll(gathered, -owner * owner_rows, axis=0)
    left = ordered_half[:all_rows].astype(jnp.float32).reshape(left_blocks, BLOCK, BLOCK)
    right_half = ordered_half[all_rows:].reshape(right_blocks, BLOCK, BLOCK)
    right = right_half.astype(jnp.float32)
    turned = jnp.einsum(
        "rbj,bjl->rbl",
        gradient[0].reshape(row_count, right_blocks, BLOCK),
        right_half,
        preferred_element_type=jnp.float32,
    )
    turned = clip_of(local_squares, entries) * turned
    outgoing = turned.reshape(row_count, fsdp_count, col_share)
    received = lax.all_to_all(outgoing, "fsdp", split_axis=1, concat_axis=0, tiled=True)
    width = received.shape[2]
    columns = received[:, 0, :].reshape(left_blocks, BLOCK, width)
    rotated = jnp.einsum("bkc,bki->cbi", columns, left, precision=HIGHEST).reshape(width, all_rows)
    count = step_number[0].astype(jnp.float32)
    first_fix = 1.0 - jnp.power(jnp.float32(BETA_ONE), count)
    second_fix = 1.0 - jnp.power(jnp.float32(BETA_TWO), count)
    first_sum = BETA_ONE * first_moment[0].astype(jnp.float32) + (1.0 - BETA_ONE) * rotated
    second_sum = (
        BETA_TWO * second_moment[0].astype(jnp.float32) + (1.0 - BETA_TWO) * rotated * rotated
    )
    direction = first_sum / first_fix / (jnp.sqrt(second_sum / second_fix) + ADAM_EPS)
    backward = jnp.einsum(
        "cbi,bki->cbk", direction.reshape(col_share, left_blocks, BLOCK), left, precision=HIGHEST
    )
    returning = backward.reshape(col_share, fsdp_count, row_count)
    received = lax.all_to_all(returning, "fsdp", split_axis=1, concat_axis=0, tiled=True)
    width = received.shape[2]
    pieces = received[:, 0, :].reshape(right_blocks, BLOCK, width)
    result = jnp.einsum("blr,bjl->rbj", pieces, right, precision=HIGHEST).reshape(width, col_count)
    return (
        result[None].astype(jnp.bfloat16),
        first_sum[None].astype(jnp.bfloat16),
        second_sum[None].astype(jnp.bfloat16),
    )


def solution(mesh):
    in_specs = (
        P("group", "fsdp", None),
        P("group", "fsdp", None),
        P("group", "fsdp", None),
        P("group", "fsdp", None),
        P(),
        P("group"),
    )
    out_specs = (P("group", "fsdp", None), P("group", "fsdp", None), P("group", "fsdp", None))
    return jax.shard_map(local, mesh=mesh, in_specs=in_specs, out_specs=out_specs, check_vma=False)
```

profile of v0, /device:TPU:0, one launch (start us, length us, event | category | flops | bytes accessed | tf_op | source)
XLA Modules:
  0.0 129.8 jit_solution(4664834779437250794)
XLA Ops:
  7.2 0.0 all-gather.3.cloned.1.call-start
  7.2 0.7 all-gather.3.cloned.1.call-update
  7.9 1.9 %multiply_reduce_fusion = f32[]{:T(128)} fusion(bf16[1,64,4096]{2,1,0:T(8,128)(2,1)} %param.6), kind=kLoop, calls=%fused_computation.24 | loop fusion | flops 786431 | bytes 524292 | tf_op jit(solution)/shard_map/reduce_sum | solution.py:33
  9.8 42.2 %psum.7 = f32[]{:T(128)} all-reduce(f32[]{:T(128)} %multiply_reduce_fusion), channel_id=1, replica_groups=mesh['fsdp'=8,'group'=4] {'fsdp','group'}, use_global_device_ids=true, to_apply=%region_1.2 | all-reduce | flops 1 | bytes 8 | tf_op jit(solution)/shard_map/psum | solution.py:18
  54.0 1.1 copy.42
  55.2 0.0 all-gather.3.cloned.1.call-done
  55.3 3.7 %fusion = bf16[4608,256]{1,0:T(8,128)(2,1)S(1)} fusion(s32[]{:T(128)S(6)} %select_n.21, bf16[4608,256]{1,0:T(8,128)(2,1)} %bitcast.46), kind=kLoop, calls=%fused_computation.2 | loop fusion | flops 4718592 | bytes 4718596 | tf_op jit(solution)/shard_map/jit(_roll_dynamic)/concatenate | solution.py:37
  58.9 0.0 copy-start
  59.0 0.1 slice.8
  59.1 0.5 fusion.1
  59.6 0.8 copy-done
  60.4 0.6 copy.30
  61.0 1.3 %reshape.80 = f32[64,8,512]{2,1,0:T(8,128)} reshape(f32[64,16,256]{2,1,0:T(8,128)S(1)} %copy.30) | data formatting | bytes 2097152 | tf_op jit(solution)/shard_map/reshape | solution.py:48
  62.3 2.8 %copy.31 = f32[64,8,512]{2,0,1:T(8,128)} copy(f32[64,8,512]{2,1,0:T(8,128)} %reshape.80) | data formatting | bytes 2097152 | tf_op jit(solution)/shard_map/reshape | solution.py:48
  65.1 3.8 %all-to-all-start = ((f32[64,8,512]{2,0,1:T(8,128)}), f32[64,8,512]{2,0,1:T(8,128)S(1)}, u32[]{:S(2)}, u32[]{:S(2)}) async-start(f32[64,8,512]{2,0,1:T(8,128)} %copy.31), calls=%async_computation | async-start | bytes 2097152 | tf_op jit(solution)/shard_map/all_to_all | solution.py:49
  68.9 1.0 slice.9
  69.9 14.4 %all-to-all-done = f32[64,8,512]{2,0,1:T(8,128)S(1)} async-done(((f32[64,8,512]{2,0,1:T(8,128)}), f32[64,8,512]{2,0,1:T(8,128)S(1)}, u32[]{:S(2)}, u32[]{:S(2)}) %all-to-all-start) | async-done | bytes 1048608 | tf_op jit(solution)/shard_map/all_to_all | solution.py:49
  84.3 1.7 %fusion.23 = f32[2,256,512]{2,1,0:T(8,128)} fusion(bf16[2,256,256]{2,1,0:T(8,128)(2,1)S(1)} %bitcast.49, f32[2,256,512]{2,1,0:T(8,128)S(1)} %bitcast.43), kind=kOutput, calls=%fused_computation.32 | convolution fusion | flops 805306368 | bytes 2359296 | tf_op jit(solution)/shard_map/bkc,bki->cbi/dot_general | solution.py:52
  85.9 2.5 %copy.38 = f32[1,512,512]{2,1,0:T(8,128)} copy(f32[1,512,512]{1,2,0:T(8,128)} %bitcast.44) | data formatting | bytes 2097152 | tf_op jit(solution)/shard_map/reshape | solution.py:52
  88.5 3.0 %fusion.14 = (bf16[1,512,512]{2,1,0:T(8,128)(2,1)}, bf16[1,512,512]{2,1,0:T(8,128)(2,1)}, f32[1,512,512]{2,1,0:T(8,128)}, f32[1,512,512]{2,1,0:T(8,128)S(1)}) fusion(f32[1,512,512]{2,1,0:T(8,128)} %copy.38, bf16[1,512,512]{2,1,0:T(8,128)(2,1)} %param.8, bf16[1,512,512]{2,1,0:T(8,128)(2,1)} %param.7), kind=kLoop, calls=%fused_computation.20 | loop fusion | flops 2621440 | bytes 5242880 | tf_op jit(solution)/shard_map/convert_element_type | solution.py:72
  91.5 2.6 %copy.28 = f32[1,512,512]{1,2,0:T(8,128)} copy(f32[1,512,512]{2,1,0:T(8,128)} %get-tuple-element.5) | data formatting | bytes 2097152 | tf_op jit(solution)/shard_map/mul | solution.py:56
  94.1 1.3 %copy.33 = f32[1,512,512]{1,2,0:T(8,128)} copy(f32[1,512,512]{2,1,0:T(8,128)S(1)} %get-tuple-element.6) | data formatting | bytes 2097152 | tf_op jit(solution)/shard_map/mul | solution.py:58
  95.4 3.1 %fusion.4 = f32[2,256,512]{2,1,0:T(8,128)S(1)} fusion(bf16[2,256,256]{2,1,0:T(8,128)(2,1)S(1)} %bitcast.50, f32[512,2,256]{0,2,1:T(8,128)} %bitcast.51, f32[512,2,256]{0,2,1:T(8,128)} %bitcast.52, f32[2,256,512]{2,1,0:T(8,128)} %fusion.23, f32[]{:T(128)} %bitcast.10), kind=kOutput, calls=%fused_computation.12 | convolution fusion | flops 807403520 | bytes 4456452 | tf_op jit(solution)/shard_map/cbi,bki->cbk/dot_general | solution.py:61
  98.6 17.8 %all_to_all.30 = f32[512,8,64]{0,2,1:T(8,128)S(1)} all-to-all(f32[512,8,64]{0,2,1:T(8,128)S(1)} %bitcast.53), channel_id=1, replica_groups=mesh['fsdp'=8,'group'=4] {'fsdp'}, dimensions={1} | all-to-all | bytes 2097152 | tf_op jit(solution)/shard_map/all_to_all | solution.py:65
  116.3 1.6 %copy.35 = f32[8,512,1,64]{1,0,3,2:T(8,128)} copy(f32[8,512,1,64]{1,3,0,2:T(8,128)S(1)} %bitcast.45) | data formatting | bytes 2097152 | tf_op jit(solution)/shard_map/all_to_all | solution.py:65
  117.9 1.4 %reshape_squeeze.11 = f32[16,256,64]{1,0,2:T(8,128)S(1)} reshape(f32[8,512,1,64]{1,0,3,2:T(8,128)} %copy.35) | data formatting | bytes 2097152 | tf_op jit(solution)/shard_map/reshape;squeeze | solution.py:67
  119.3 2.3 %fusion.2 = bf16[64,16,256]{2,0,1:T(8,128)(2,1)S(1)} fusion(bf16[16,256,256]{2,1,0:T(8,128)(2,1)S(1)} %bitcast.42, f32[16,256,64]{1,0,2:T(8,128)S(1)} %reshape_squeeze.11), kind=kOutput, calls=%fused_computation.10 | convolution fusion | flops 805568512 | bytes 3670016 | tf_op jit(solution)/shard_map/blr,bjl->rbj/dot_general | solution.py:68
  121.6 0.3 copy.37
  121.9 1.0 convert_element_type.55
Async XLA Ops:
  7.2 48.1 %all-gather.3.cloned.1.call-start = ((), (), s32[]{:S(2)}) async-start(), calls=%async_computation.2 | async-start | bytes 2654208 | tf_op jit(solution)/shard_map/all_gather | solution.py:34
  58.9 1.4 %copy-start = (bf16[4608,256]{1,0:T(8,128)(2,1)}, bf16[4608,256]{1,0:T(8,128)(2,1)S(1)}, u32[]{:S(2)}) copy-start(bf16[4608,256]{1,0:T(8,128)(2,1)S(1)} %fusion) | copy-start | bytes 7077892
  65.1 19.2 %all-to-all-start = ((f32[64,8,512]{2,0,1:T(8,128)}), f32[64,8,512]{2,0,1:T(8,128)S(1)}, u32[]{:S(2)}, u32[]{:S(2)}) async-start(f32[64,8,512]{2,0,1:T(8,128)} %copy.31), calls=%async_computation | async-start | bytes 2097152 | tf_op jit(solution)/shard_map/all_to_all | solution.py:49
Sparse Core Ops, SparseCore 0:
  9.9 31.9 all-gather.2
where the time goes:
time: 130 us
  blocking collectives  60 us (46%)
  local copies, waits for them, and re-layouts  18.5 us (14%)
  between operations  16.2 us (12%)
  waiting for transfers between devices  15.1 us (12%)
  other arithmetic  8.61 us (7%)
  matrix products  7.53 us (6%)
  starting transfers between devices  3.82 us (3%)
    psum x1, blocking collectives, clip_of(): total = lax.psum(local_squares, ('fsdp', 'group'))  42.2 us
    all_to_all x1, blocking collectives, local(): lax.all_to_all(returning, 'fsdp', split_axis=1, concat_axis=0, tiled=True)  17.8 us
    all_to_all x1, waiting for transfers between devices, local(): lax.all_to_all(outgoing, 'fsdp', split_axis=1, concat_axis=0, tiled=True)  14.4 us
    reshape x2, local copies, waits for them, and re-layouts, local(): outgoing = turned.reshape(row_count, fsdp_count, col_share)  4.1 us
    all_to_all x1, starting transfers between devices, local(): lax.all_to_all(outgoing, 'fsdp', split_axis=1, concat_axis=0, tiled=True)  3.79 us
    concatenate x1, other arithmetic, local(): ordered_half = jnp.roll(gathered, -owner * owner_rows, axis=0)  3.67 us
    dot_general x1, matrix products, local(): jnp.einsum('cbi,bki->cbk', direction.reshape(col_share, left_blocks, BLOC...  3.12 us
    convert_element_type x1, other arithmetic, local(): second_sum[None].astype(jnp.bfloat16)  3.02 us
  transfers between devices with their start and end apart: 2, of which 1 were waited for; matrix products, arithmetic and copies ran while one was open for 3% of the time, Pallas kernels for 0%

commit v1 on v0

--- a/solution.py
+++ b/solution.py
@@ -1,8 +1,11 @@
+import functools
 import math
 
 import jax
 import jax.numpy as jnp
 from jax import lax
+from jax.experimental import pallas as pl
+from jax.experimental.pallas import tpu as pltpu
 from jax.sharding import PartitionSpec as P
 
 BLOCK = 256
@@ -19,7 +22,7 @@
     return jnp.float32(math.sqrt(entries)) / (jnp.sqrt(total) + 1e-06)
 
 
-def local(gradient, first_moment, second_moment, basis_store, step_number, matrix_ids):
+def local_general(gradient, first_moment, second_moment, basis_store, step_number, matrix_ids):
     fsdp_count = lax.axis_size("fsdp")
     group_count = lax.axis_size("group")
     row_count = gradient.shape[1]
@@ -73,6 +76,310 @@
     )
 
 
+SLAB = 16
+LANES = 128
+MESH = pl.DeviceIdType.MESH
+
+
+def pieces_of(x):
+    high = x.astype(jnp.bfloat16)
+    rest = x - high.astype(jnp.float32)
+    middle = rest.astype(jnp.bfloat16)
+    low = (rest - middle.astype(jnp.float32)).astype(jnp.bfloat16)
+    return high, middle, low
+
+
+def mm(a, b, dims):
+    return lax.dot_general(a, b, (dims, ((), ())), preferred_element_type=jnp.float32)
+
+
+NN = ((1,), (0,))
+NT = ((1,), (1,))
+
+
+def kernel(n, groups, grad, first, second, basis, step, ident, out_u, out_1, out_2,
+           own, m1, m2, hop, staged, left, right, got, n1, n2, upd, sq_own, sq_z, sq_mid, sq_f,
+           loc, hop_s, hop_r, left_s, left_r, right_s, right_r, got_s, got_r,
+           ret_s, ret_r, z_s, z_r, f_s, f_r):
+    me = lax.axis_index("fsdp")
+    zz = lax.axis_index("group")
+    share = grad.shape[1]
+    cols = grad.shape[2]
+    width = cols // n
+    halves = width // BLOCK
+    slabs = n // 2
+    per_owner = basis.shape[0]
+    span = slabs * SLAB
+    left_groups = left.shape[0]
+    block_groups = BLOCK // span
+    entries = float(share * n * cols * groups)
+
+    def peer(k):
+        return lax.rem(me + k, n)
+
+    def zpeer(k):
+        return lax.rem(zz + k, groups)
+
+    def lanes_of(c):
+        return pl.ds(pl.multiple_of(lax.rem(c, 2) * LANES, LANES), LANES)
+
+    def rows_of(c):
+        return pl.ds(pl.multiple_of((c // 2) * SLAB, SLAB), SLAB)
+
+    def share_rows(d):
+        return pl.ds(pl.multiple_of(d * share, share), share)
+
+    def out_cols(d, t):
+        return pl.ds(pl.multiple_of(d * width + t * BLOCK, BLOCK), BLOCK)
+
+    def remote(src, dst, ssem, rsem, k):
+        return pltpu.make_async_remote_copy(
+            src_ref=src, dst_ref=dst, send_sem=ssem, recv_sem=rsem,
+            device_id={"fsdp": peer(k)}, device_id_type=MESH)
+
+    locals_ = [
+        pltpu.make_async_copy(grad.at[0], own, loc.at[0]),
+        pltpu.make_async_copy(basis.at[:, me // 2, :, lanes_of(me)], hop.at[me], loc.at[1]),
+        pltpu.make_async_copy(first.at[0], m1, loc.at[2]),
+        pltpu.make_async_copy(second.at[0], m2, loc.at[3]),
+    ]
+    for t in range(halves):
+        locals_.append(pltpu.make_async_copy(
+            grad.at[0, :, out_cols(me, t)], got.at[t, share_rows(me)], loc.at[4 + t]))
+    for copy in locals_:
+        copy.start()
+
+    barrier = pltpu.get_barrier_semaphore()
+    for k in range(1, n):
+        pl.semaphore_signal(barrier, inc=1, device_id={"fsdp": peer(k)}, device_id_type=MESH)
+    for k in range(1, groups):
+        pl.semaphore_signal(barrier, inc=1, device_id={"group": zpeer(k)}, device_id_type=MESH)
+    pl.semaphore_wait(barrier, n - 1 + groups - 1)
+
+    hops = []
+    for k in range(1, n):
+        c = peer(k)
+        hops.append(remote(basis.at[:, c // 2, :, lanes_of(c)], hop.at[me],
+                           hop_s.at[k], hop_r.at[k], k))
+        hops[-1].start()
+
+    gots = [[None] * n for _ in range(halves)]
+
+    def send_got(t):
+        for k in range(1, n):
+            gots[t][k] = remote(grad.at[0, :, out_cols(peer(k), t)], got.at[t, share_rows(me)],
+                                got_s.at[t, k], got_r.at[t, k], k)
+            gots[t][k].start()
+
+    send_got(0)
+
+    locals_[0].wait()
+    squares = jnp.zeros((8, LANES), jnp.float32)
+    for r in range(0, share, 16):
+        rows = own[r:r + 16, :].astype(jnp.float32)
+        rows = rows * rows
+        rows = rows[0:8] + rows[8:16]
+        for c in range(0, cols, LANES):
+            squares = squares + rows[:, c:c + LANES]
+    sq_own[...] = squares
+    zs = []
+    for k in range(1, groups):
+        zs.append(pltpu.make_async_remote_copy(
+            src_ref=sq_own, dst_ref=sq_z.at[k], send_sem=z_s.at[k], recv_sem=z_r.at[k],
+            device_id={"group": zpeer(k)}, device_id_type=MESH))
+        zs[-1].start()
+
+    for copy in hops:
+        copy.wait_recv()
+    locals_[1].wait()
+    owner = lax.rem(step[0] + ident[0], n)
+    for q in range(n):
+        staged[q * per_owner:(q + 1) * per_owner] = hop[lax.rem(owner + q, n)]
+
+    rights = [[None] * n for _ in range(halves)]
+
+    def send_right(t):
+        for k in range(n):
+            d = peer(k)
+            src = staged.at[pl.ds(left_groups + (d * halves + t) * block_groups, block_groups)]
+            dst = right.at[t, :, rows_of(me), lanes_of(me)]
+            if k == 0:
+                rights[t][k] = pltpu.make_async_copy(src, dst, right_r.at[t, 0])
+            else:
+                rights[t][k] = remote(src, dst, right_s.at[t, k], right_r.at[t, k], k)
+            rights[t][k].start()
+
+    send_right(0)
+    lefts = []
+    for k in range(n):
+        src = staged.at[pl.ds(0, left_groups)]
+        dst = left.at[:, rows_of(me), lanes_of(me)]
+        if k == 0:
+            lefts.append(pltpu.make_async_copy(src, dst, left_r.at[0]))
+        else:
+            lefts.append(remote(src, dst, left_s.at[k], left_r.at[k], k))
+        lefts[-1].start()
+    for t in range(1, halves):
+        send_got(t)
+        send_right(t)
+
+    squares = sq_own[...]
+    for k, copy in enumerate(zs):
+        copy.wait_recv()
+        squares = squares + sq_z[k + 1]
+    sq_mid[...] = squares
+    fs = []
+    for k in range(1, n):
+        fs.append(remote(sq_mid, sq_f.at[k], f_s.at[k], f_r.at[k], k))
+        fs[-1].start()
+    for k, copy in enumerate(fs):
+        copy.wait_recv()
+        squares = squares + sq_f[k + 1]
+    total = jnp.sum(squares, keepdims=True)
+    clip = jnp.float32(math.sqrt(entries)) / (jnp.sqrt(total) + 1e-06)
+    count = jnp.full((1, 1), step[0].astype(jnp.float32))
+    first_inv = 1.0 / (1.0 - jnp.exp(count * jnp.float32(math.log(BETA_ONE))))
+    second_inv = 1.0 / (1.0 - jnp.exp(count * jnp.float32(math.log(BETA_TWO))))
+
+    locals_[2].wait()
+    locals_[3].wait()
+    all_rows = share * n
+    left_blocks = all_rows // BLOCK
+    returns = []
+    outs = []
+    for t in range(halves):
+        for copy in rights[t][1:]:
+            copy.wait_recv()
+        rights[t][0].wait()
+        if t == 0:
+            for copy in lefts[1:]:
+                copy.wait_recv()
+            lefts[0].wait()
+        for k in range(1, n):
+            gots[t][k].wait_recv()
+        locals_[4 + t].wait()
+        rt = right[t].reshape(BLOCK, BLOCK)
+        flipped = rt.astype(jnp.float32).T.astype(jnp.bfloat16)
+        cut = slice(t * BLOCK, (t + 1) * BLOCK)
+        for b in range(left_blocks):
+            cols_b = slice(b * BLOCK, (b + 1) * BLOCK)
+            lb = left[b * block_groups:(b + 1) * block_groups].reshape(BLOCK, BLOCK)
+            turned = mm(flipped, got[t, cols_b, :], NT)
+            rotated = sum(mm(piece, lb, NN) for piece in pieces_of(turned)) * clip
+            first_sum = BETA_ONE * m1[cut, cols_b].astype(jnp.float32) + (1.0 - BETA_ONE) * rotated
+            second_sum = (BETA_TWO * m2[cut, cols_b].astype(jnp.float32)
+                          + (1.0 - BETA_TWO) * rotated * rotated)
+            n1[cut, cols_b] = first_sum.astype(jnp.bfloat16)
+            n2[cut, cols_b] = second_sum.astype(jnp.bfloat16)
+            direction = first_sum * first_inv / (jnp.sqrt(second_sum * second_inv) + ADAM_EPS)
+            back = sum(mm(rt, piece, NN) for piece in pieces_of(direction))
+            result = sum(mm(lb, piece, NT) for piece in pieces_of(back))
+            upd[t, cols_b, :] = result.astype(jnp.bfloat16)
+        for k in range(n):
+            src = upd.at[t, share_rows(peer(k))]
+            dst = out_u.at[0, :, out_cols(me, t)]
+            if k == 0:
+                copy = pltpu.make_async_copy(src, dst, ret_r.at[t, 0])
+                outs.append(copy)
+            else:
+                copy = remote(src, dst, ret_s.at[t, k], ret_r.at[t, k], k)
+                returns.append(copy)
+            copy.start()
+        for index, (value, target) in enumerate(((n1, out_1), (n2, out_2))):
+            copy = pltpu.make_async_copy(
+                value.at[cut], target.at[0, cut], loc.at[4 + halves + 2 * t + index])
+            copy.start()
+            outs.append(copy)
+
+    for copy in hops + zs + fs + lefts[1:]:
+        copy.wait_send()
+    for t in range(halves):
+        for k in range(1, n):
+            gots[t][k].wait_send()
+            rights[t][k].wait_send()
+    for copy in outs:
+        copy.wait()
+    for copy in returns:
+        copy.wait()
+
+
+def fits(gradient, first_moment, basis_store, n):
+    if n % 2:
+        return False
+    span = n // 2 * SLAB
+    width = gradient.shape[2] // n
+    all_rows = gradient.shape[1] * n
+    return (
+        BLOCK % span == 0
+        and basis_store.shape[1] % span == 0
+        and width % BLOCK == 0
+        and all_rows % BLOCK == 0
+        and gradient.shape[1] % SLAB == 0
+        and all_rows <= 1024
+        and width <= 1024
+    )
+
+
+def local(gradient, first_moment, second_moment, basis_store, step_number, matrix_ids):
+    n = lax.axis_size("fsdp")
+    groups = lax.axis_size("group")
+    if not fits(gradient, first_moment, basis_store, n):
+        return local_general(
+            gradient, first_moment, second_moment, basis_store, step_number, matrix_ids
+        )
+    share, cols = gradient.shape[1:]
+    all_rows = share * n
+    width = cols // n
+    halves = width // BLOCK
+    slabs = n // 2
+    span = slabs * SLAB
+    per_owner = basis_store.shape[1] // span
+    basis = basis_store.reshape(per_owner, slabs, SLAB, BLOCK)
+    half = jnp.bfloat16
+    anywhere = pl.BlockSpec(memory_space=pl.ANY)
+    scalar = pl.BlockSpec(memory_space=pltpu.SMEM)
+    dma = pltpu.SemaphoreType.DMA
+    tile = (8, LANES)
+    return pl.pallas_call(
+        functools.partial(kernel, n, groups),
+        out_shape=(
+            jax.ShapeDtypeStruct(gradient.shape, half),
+            jax.ShapeDtypeStruct(first_moment.shape, half),
+            jax.ShapeDtypeStruct(second_moment.shape, half),
+        ),
+        in_specs=[anywhere] * 4 + [scalar] * 2,
+        out_specs=(anywhere,) * 3,
+        scratch_shapes=[
+            pltpu.VMEM((share, cols), half),
+            pltpu.VMEM((width, all_rows), half),
+            pltpu.VMEM((width, all_rows), half),
+            pltpu.VMEM((n, per_owner, SLAB, LANES), half),
+            pltpu.VMEM((n * per_owner, SLAB, LANES), half),
+            pltpu.VMEM((all_rows // span, span, BLOCK), half),
+            pltpu.VMEM((halves, BLOCK // span, span, BLOCK), half),
+            pltpu.VMEM((halves, all_rows, BLOCK), half),
+            pltpu.VMEM((width, all_rows), half),
+            pltpu.VMEM((width, all_rows), half),
+            pltpu.VMEM((halves, all_rows, BLOCK), half),
+            pltpu.VMEM(tile, jnp.float32),
+            pltpu.VMEM((groups,) + tile, jnp.float32),
+            pltpu.VMEM(tile, jnp.float32),
+            pltpu.VMEM((n,) + tile, jnp.float32),
+            dma((4 + 3 * halves,)),
+            dma((n,)), dma((n,)),
+            dma((n,)), dma((n,)),
+            dma((halves, n)), dma((halves, n)),
+            dma((halves, n)), dma((halves, n)),
+            dma((halves, n)), dma((halves, n)),
+            dma((groups,)), dma((groups,)),
+            dma((n,)), dma((n,)),
+        ],
+        compiler_params=pltpu.CompilerParams(
+            collective_id=0, has_side_effects=True, vmem_limit_bytes=32 << 20
+        ),
+    )(gradient, first_moment, second_moment, basis, step_number, matrix_ids)
+
+
 def solution(mesh):
     in_specs = (
         P("group", "fsdp", None),

time: 130 us -> 42.8 us (0.33)
  blocking collectives: 60 us -> 0 us
  Pallas kernels: 0 us -> 34.1 us
  waiting for transfers between devices: 15.1 us -> 0 us
  between operations: 16.2 us -> 1.94 us
  local copies, waits for them, and re-layouts: 18.5 us -> 6.46 us
  other arithmetic: 8.61 us -> 0 us
  matrix products: 7.53 us -> 0 us
  starting transfers between devices: 3.82 us -> 0 us
    psum x1 -> x0, blocking collectives: 42.2 us -> none  [clip_of(): total = lax.psum(local_squares, ('fsdp', 'group'))]
    pallas_call x0 -> x1, Pallas kernels: none -> 34.1 us  [local(): pl.pallas_call(functools.partial(kernel, n, groups), out_shape=(jax.Shape...]
    all_to_all x1 -> x0, blocking collectives: 17.8 us -> none  [local(): lax.all_to_all(returning, 'fsdp', split_axis=1, concat_axis=0, tiled=True)]
    all_to_all x1 -> x0, waiting for transfers between devices: 14.4 us -> none  [local(): lax.all_to_all(outgoing, 'fsdp', split_axis=1, concat_axis=0, tiled=True)]
    dot_general x4 -> x0, matrix products: 7.53 us -> none  [the longest x1 3.12 us: local(): jnp.einsum('cbi,bki->cbk', direction.reshape(col_share, left_blocks, BLOC...]
    reshape x3 -> x0, local copies, waits for them, and re-layouts: 6.65 us -> none  [the longest x2 4.1 us: local(): outgoing = turned.reshape(row_count, fsdp_count, col_share)]
    mul x3 -> x0, local copies, waits for them, and re-layouts: 4.52 us -> none  [the longest x1 2.59 us: local(): BETA_ONE * first_moment[0].astype(jnp.float32) + (1.0 - BETA_ONE) * rotated]
    unnamed x3 -> x11, local copies, waits for them, and re-layouts: 1.95 us -> 6.46 us
  transfers between devices with their start and end apart: 2 -> 0, of which waited for: 1 -> 0; matrix products, arithmetic and copies ran while one was open for 3% -> 0% of each run, Pallas kernels for 0% -> 0%
where the time goes in v1:
time: 42.8 us; the launch traced here: 42.5 us
  Pallas kernels  34.1 us (80%)
  local copies, waits for them, and re-layouts  6.46 us (15%)
  between operations  1.94 us (5%)
    pallas_call x1, Pallas kernels, local(): pl.pallas_call(functools.partial(kernel, n, groups), out_shape=(jax.Shape...  34.1 us
    unnamed x11, local copies, waits for them, and re-layouts  6.46 us

profile of v1, /device:TPU:0, one launch (start us, length us, event | category | flops | bytes accessed | tf_op | source)
XLA Modules:
  0.0 42.5 jit_solution(17166590666869664945)
XLA Ops:
  1.9 0.0 copy-start
  1.9 1.0 %copy-done = bf16[1,64,4096]{2,1,0:T(8,128)(2,1)S(1)} copy-done((bf16[1,64,4096]{2,1,0:T(8,128)(2,1)S(1)}, bf16[1,64,4096]{2,1,0:T(8,128)(2,1)}, u32[]{:S(2)}) %copy-start) | copy-done | bytes 524312
  3.0 0.0 copy-start.1
  3.0 1.0 %copy-done.1 = bf16[1,512,512]{2,1,0:T(8,128)(2,1)S(1)} copy-done((bf16[1,512,512]{2,1,0:T(8,128)(2,1)S(1)}, bf16[1,512,512]{2,1,0:T(8,128)(2,1)}, u32[]{:S(2)}) %copy-start.1) | copy-done | bytes 524312
  4.0 0.0 copy-start.2
  4.0 1.0 %copy-done.2 = bf16[1,512,512]{2,1,0:T(8,128)(2,1)S(1)} copy-done((bf16[1,512,512]{2,1,0:T(8,128)(2,1)S(1)}, bf16[1,512,512]{2,1,0:T(8,128)(2,1)}, u32[]{:S(2)}) %copy-start.2) | copy-done | bytes 524312
  5.0 0.0 copy-start.3
  5.1 1.0 %copy-done.3 = bf16[1,576,256]{2,1,0:T(8,128)(2,1)S(1)} copy-done((bf16[1,576,256]{2,1,0:T(8,128)(2,1)S(1)}, bf16[1,576,256]{2,1,0:T(8,128)(2,1)}, u32[]{:S(2)}) %copy-start.3) | copy-done | bytes 294936
  6.0 34.1 %shard_map.85 = (bf16[1,64,4096]{2,1,0:T(8,128)(2,1)S(1)}, bf16[1,512,512]{2,1,0:T(8,128)(2,1)S(1)}, bf16[1,512,512]{2,1,0:T(8,128)(2,1)S(1)}) custom-call(bf16[1,64,4096]{2,1,0:T(8,128)(2,1)S(1)} %copy-done, bf16[1,512,512]{2,1,0:T(8,128)(2,1)S(1)} %copy-done.1, bf16[1,512,512]{2,1,0:T(8,128)(2,1)S(1)} %copy-done.2, bf16[9,4,16,256]{3,2,1,0:T(8,128)(2,1)S(1)} %bitcast.1, ...), custom_call_target="tpu_custom_call" | custom-call | tf_op jit(solution)/shard_map/pallas_call | solution.py:343
  40.1 0.8 %copy.14 = bf16[1,64,4096]{2,1,0:T(8,128)(2,1)} copy(bf16[1,64,4096]{2,1,0:T(8,128)(2,1)S(1)} %get-tuple-element.6) | data formatting | bytes 1048576
  40.9 0.8 %copy.15 = bf16[1,512,512]{2,1,0:T(8,128)(2,1)} copy(bf16[1,512,512]{2,1,0:T(8,128)(2,1)S(1)} %get-tuple-element.7) | data formatting | bytes 1048576
  41.7 0.8 %copy.16 = bf16[1,512,512]{2,1,0:T(8,128)(2,1)} copy(bf16[1,512,512]{2,1,0:T(8,128)(2,1)S(1)} %get-tuple-element.8) | data formatting | bytes 1048576
Async XLA Ops:
  1.9 1.0 %copy-start = (bf16[1,64,4096]{2,1,0:T(8,128)(2,1)S(1)}, bf16[1,64,4096]{2,1,0:T(8,128)(2,1)}, u32[]{:S(2)}) copy-start(bf16[1,64,4096]{2,1,0:T(8,128)(2,1)} %grad.1) | copy-start | bytes 1572868
  3.0 1.0 %copy-start.1 = (bf16[1,512,512]{2,1,0:T(8,128)(2,1)S(1)}, bf16[1,512,512]{2,1,0:T(8,128)(2,1)}, u32[]{:S(2)}) copy-start(bf16[1,512,512]{2,1,0:T(8,128)(2,1)} %first.1) | copy-start | bytes 1572868
  4.0 1.0 %copy-start.2 = (bf16[1,512,512]{2,1,0:T(8,128)(2,1)S(1)}, bf16[1,512,512]{2,1,0:T(8,128)(2,1)}, u32[]{:S(2)}) copy-start(bf16[1,512,512]{2,1,0:T(8,128)(2,1)} %second.1) | copy-start | bytes 1572868
  5.0 1.0 %copy-start.3 = (bf16[1,576,256]{2,1,0:T(8,128)(2,1)S(1)}, bf16[1,576,256]{2,1,0:T(8,128)(2,1)}, u32[]{:S(2)}) copy-start(bf16[1,576,256]{2,1,0:T(8,128)(2,1)} %param.9) | copy-start | bytes 884740

commit v2 on v1

--- a/solution.py
+++ b/solution.py
@@ -171,8 +171,6 @@
                                 got_s.at[t, k], got_r.at[t, k], k)
             gots[t][k].start()
 
-    send_got(0)
-
     locals_[0].wait()
     squares = jnp.zeros((8, LANES), jnp.float32)
     for r in range(0, share, 16):
@@ -189,6 +187,18 @@
             device_id={"group": zpeer(k)}, device_id_type=MESH))
         zs[-1].start()
 
+    send_got(0)
+
+    squares = sq_own[...]
+    for k, copy in enumerate(zs):
+        copy.wait_recv()
+        squares = squares + sq_z[k + 1]
+    sq_mid[...] = squares
+    fs = []
+    for k in range(1, n):
+        fs.append(remote(sq_mid, sq_f.at[k], f_s.at[k], f_r.at[k], k))
+        fs[-1].start()
+
     for copy in hops:
         copy.wait_recv()
     locals_[1].wait()
@@ -223,15 +233,7 @@
         send_got(t)
         send_right(t)
 
-    squares = sq_own[...]
-    for k, copy in enumerate(zs):
-        copy.wait_recv()
-        squares = squares + sq_z[k + 1]
-    sq_mid[...] = squares
-    fs = []
-    for k in range(1, n):
-        fs.append(remote(sq_mid, sq_f.at[k], f_s.at[k], f_r.at[k], k))
-        fs[-1].start()
+    squares = sq_mid[...]
     for k, copy in enumerate(fs):
         copy.wait_recv()
         squares = squares + sq_f[k + 1]
@@ -303,6 +305,30 @@
         copy.wait()
 
 
+def hbm(x):
+    return pltpu.with_memory_space_constraint(x, pltpu.MemorySpace.HBM)
+
+
+def copy_kernel(a, b, c, x, y, z, sems):
+    copies = [pltpu.make_async_copy(src, dst, sems.at[i])
+              for i, (src, dst) in enumerate(((a, x), (b, y), (c, z)))]
+    for copy in copies:
+        copy.start()
+    for copy in copies:
+        copy.wait()
+
+
+def place(arrays):
+    return pl.pallas_call(
+        copy_kernel,
+        out_shape=tuple(jax.ShapeDtypeStruct(a.shape, a.dtype) for a in arrays),
+        in_specs=[pl.BlockSpec(memory_space=pltpu.VMEM)] * 3,
+        out_specs=(pl.BlockSpec(memory_space=pl.ANY),) * 3,
+        scratch_shapes=[pltpu.SemaphoreType.DMA((3,))],
+        compiler_params=pltpu.CompilerParams(vmem_limit_bytes=8 << 20),
+    )(*arrays)
+
+
 def fits(gradient, first_moment, basis_store, n):
     if n % 2:
         return False
@@ -340,7 +366,7 @@
     scalar = pl.BlockSpec(memory_space=pltpu.SMEM)
     dma = pltpu.SemaphoreType.DMA
     tile = (8, LANES)
-    return pl.pallas_call(
+    results = pl.pallas_call(
         functools.partial(kernel, n, groups),
         out_shape=(
             jax.ShapeDtypeStruct(gradient.shape, half),
@@ -377,7 +403,8 @@
         compiler_params=pltpu.CompilerParams(
             collective_id=0, has_side_effects=True, vmem_limit_bytes=32 << 20
         ),
-    )(gradient, first_moment, second_moment, basis, step_number, matrix_ids)
+    )(*[hbm(x) for x in (gradient, first_moment, second_moment, basis)], step_number, matrix_ids)
+    return place(results)
 
 
 def solution(mesh):

time: 42.8 us -> 34 us (0.79)
  local copies, waits for them, and re-layouts: 6.46 us -> 0 us
  Pallas kernels: 34.1 us -> 31.9 us
    unnamed x11 -> x0, local copies, waits for them, and re-layouts: 6.46 us -> none
    pallas_call x1, Pallas kernels: 34.1 us -> 30.7 us  [local(): pl.pallas_call(functools.partial(kernel, n, groups), out_shape=(jax.Shape...]
    pallas_call x0 -> x1, Pallas kernels: none -> 1.17 us  [place(): pl.pallas_call(copy_kernel, out_shape=tuple((jax.ShapeDtypeStruct(a.shape...]
where the time goes in v2:
time: 34 us; the launch traced here: 33.8 us
  Pallas kernels  31.9 us (94%)
  between operations  1.93 us (6%)
    pallas_call x1, Pallas kernels, local(): pl.pallas_call(functools.partial(kernel, n, groups), out_shape=(jax.Shape...  30.7 us
    pallas_call x1, Pallas kernels, place(): pl.pallas_call(copy_kernel, out_shape=tuple((jax.ShapeDtypeStruct(a.shape...  1.17 us

profile of v2, /device:TPU:0, one launch (start us, length us, event | category | flops | bytes accessed | tf_op | source)
XLA Modules:
  0.0 33.8 jit_solution(13231978994868307323)
XLA Ops:
  1.9 30.7 %shard_map.85 = (bf16[1,64,4096]{2,1,0:T(8,128)(2,1)S(1)}, bf16[1,512,512]{2,1,0:T(8,128)(2,1)S(1)}, bf16[1,512,512]{2,1,0:T(8,128)(2,1)S(1)}) custom-call(bf16[1,64,4096]{2,1,0:T(8,128)(2,1)} %grad.1, bf16[1,512,512]{2,1,0:T(8,128)(2,1)} %first.1, bf16[1,512,512]{2,1,0:T(8,128)(2,1)} %second.1, bf16[9,4,16,256]{3,2,1,0:T(8,128)(2,1)} %bitcast.1, ...), custom_call_target="tpu_custom_call" | custom-call | tf_op jit(solution)/shard_map/pallas_call | solution.py:369
  32.7 1.2 %shard_map.86 = (bf16[1,64,4096]{2,1,0:T(8,128)(2,1)}, bf16[1,512,512]{2,1,0:T(8,128)(2,1)}, bf16[1,512,512]{2,1,0:T(8,128)(2,1)}) custom-call(bf16[1,64,4096]{2,1,0:T(8,128)(2,1)S(1)} %get-tuple-element.6.a, bf16[1,512,512]{2,1,0:T(8,128)(2,1)S(1)} %get-tuple-element.7.b, bf16[1,512,512]{2,1,0:T(8,128)(2,1)S(1)} %get-tuple-element.8.c), custom_call_target="tpu_custom_call" | custom-call | tf_op jit(solution)/shard_map/pallas_call | solution.py:322

commit v3 on v2

--- a/solution.py
+++ b/solution.py
@@ -78,6 +78,7 @@
 
 SLAB = 16
 LANES = 128
+PARTS = 1
 MESH = pl.DeviceIdType.MESH
 
 
@@ -111,11 +112,27 @@
     per_owner = basis.shape[0]
     span = slabs * SLAB
     left_groups = left.shape[0]
+    all_rows = share * n
+    left_blocks = all_rows // BLOCK
     block_groups = BLOCK // span
     entries = float(share * n * cols * groups)
 
-    def peer(k):
-        return lax.rem(me + k, n)
+    core = lax.rem(me, 2)
+    per = n // left_blocks
+    masks = [m for m in range(2, n, 2)] + [m for m in range(3, n, 2)]
+    swapped = [masks[i + 1] if i % 2 == 0 and i + 1 < len(masks) else masks[i - i % 2] for i in range(len(masks))]
+    order = list(zip(masks, swapped)) + [(1, 1)]
+
+    def peer(m):
+        other = me
+        for bit in (1 << i for i in range(n.bit_length() - 1)):
+            if m & bit:
+                other = other + bit * (1 - 2 * lax.rem(me // bit, 2))
+        return other
+
+    def pick(pair):
+        a, b = pair
+        return a + core * (b - a), peer(a) + core * (peer(b) - peer(a))
 
     def zpeer(k):
         return lax.rem(zz + k, groups)
@@ -132,10 +149,10 @@
     def out_cols(d, t):
         return pl.ds(pl.multiple_of(d * width + t * BLOCK, BLOCK), BLOCK)
 
-    def remote(src, dst, ssem, rsem, k):
+    def remote(src, dst, ssem, rsem, d):
         return pltpu.make_async_remote_copy(
             src_ref=src, dst_ref=dst, send_sem=ssem, recv_sem=rsem,
-            device_id={"fsdp": peer(k)}, device_id_type=MESH)
+            device_id={"fsdp": d}, device_id_type=MESH)
 
     locals_ = [
         pltpu.make_async_copy(grad.at[0], own, loc.at[0]),
@@ -156,20 +173,34 @@
         pl.semaphore_signal(barrier, inc=1, device_id={"group": zpeer(k)}, device_id_type=MESH)
     pl.semaphore_wait(barrier, n - 1 + groups - 1)
 
-    hops = []
-    for k in range(1, n):
-        c = peer(k)
-        hops.append(remote(basis.at[:, c // 2, :, lanes_of(c)], hop.at[me],
-                           hop_s.at[k], hop_r.at[k], k))
-        hops[-1].start()
-
-    gots = [[None] * n for _ in range(halves)]
+    def hop_copy(m, d):
+        return remote(basis.at[:, d // 2, :, lanes_of(d)], hop.at[me], hop_s.at[m], hop_r.at[m], d)
+
+    def got_copy(t, m, d):
+        return remote(grad.at[0, :, out_cols(d, t)], got.at[t, share_rows(me)],
+                      got_s.at[t, m], got_r.at[t, m], d)
+
+    def right_copy(t, m, d):
+        src = staged.at[pl.ds(left_groups + (d * halves + t) * block_groups, block_groups)]
+        dst = right.at[t, :, rows_of(me), lanes_of(me)]
+        return remote(src, dst, right_s.at[t, m], right_r.at[t, m], d)
+
+    def left_copy(m, d):
+        return remote(staged.at[pl.ds(0, left_groups)], left.at[:, rows_of(me), lanes_of(me)],
+                      left_s.at[m], left_r.at[m], d)
+
+    for pair in order:
+        hop_copy(*pick(pair)).start()
+    hops = [hop_copy(m, peer(m)) for m in range(1, n)]
+    gots = [[None] + [got_copy(t, m, peer(m)) for m in range(1, n)] for t in range(halves)]
+    rights = [[None] + [right_copy(t, m, peer(m)) for m in range(1, n)] for t in range(halves)]
+    lefts = [left_copy(m, peer(m)) for m in range(2, n, 2)]
+    shared = left.at[:, :, lanes_of(me)]
+    sibling = remote(shared, shared, left_s.at[1], left_r.at[1], peer(1))
 
     def send_got(t):
-        for k in range(1, n):
-            gots[t][k] = remote(grad.at[0, :, out_cols(peer(k), t)], got.at[t, share_rows(me)],
-                                got_s.at[t, k], got_r.at[t, k], k)
-            gots[t][k].start()
+        for pair in order:
+            got_copy(t, *pick(pair)).start()
 
     locals_[0].wait()
     squares = jnp.zeros((8, LANES), jnp.float32)
@@ -196,7 +227,7 @@
     sq_mid[...] = squares
     fs = []
     for k in range(1, n):
-        fs.append(remote(sq_mid, sq_f.at[k], f_s.at[k], f_r.at[k], k))
+        fs.append(remote(sq_mid, sq_f.at[k], f_s.at[k], f_r.at[k], peer(k)))
         fs[-1].start()
 
     for copy in hops:
@@ -206,29 +237,23 @@
     for q in range(n):
         staged[q * per_owner:(q + 1) * per_owner] = hop[lax.rem(owner + q, n)]
 
-    rights = [[None] * n for _ in range(halves)]
+    own_left = pltpu.make_async_copy(
+        staged.at[pl.ds(0, left_groups)], left.at[:, rows_of(me), lanes_of(me)], left_r.at[0])
+    own_left.start()
+    own_rights = [pltpu.make_async_copy(
+        staged.at[pl.ds(left_groups + (me * halves + t) * block_groups, block_groups)],
+        right.at[t, :, rows_of(me), lanes_of(me)], right_r.at[t, 0]) for t in range(halves)]
+    for copy in own_rights:
+        copy.start()
+    lefts_order = [m for m in order if m[0] % 2 == 0]
+    for m, _ in lefts_order:
+        left_copy(m, peer(m)).start()
 
     def send_right(t):
-        for k in range(n):
-            d = peer(k)
-            src = staged.at[pl.ds(left_groups + (d * halves + t) * block_groups, block_groups)]
-            dst = right.at[t, :, rows_of(me), lanes_of(me)]
-            if k == 0:
-                rights[t][k] = pltpu.make_async_copy(src, dst, right_r.at[t, 0])
-            else:
-                rights[t][k] = remote(src, dst, right_s.at[t, k], right_r.at[t, k], k)
-            rights[t][k].start()
+        for pair in order:
+            right_copy(t, *pick(pair)).start()
 
     send_right(0)
-    lefts = []
-    for k in range(n):
-        src = staged.at[pl.ds(0, left_groups)]
-        dst = left.at[:, rows_of(me), lanes_of(me)]
-        if k == 0:
-            lefts.append(pltpu.make_async_copy(src, dst, left_r.at[0]))
-        else:
-            lefts.append(remote(src, dst, left_s.at[k], left_r.at[k], k))
-        lefts[-1].start()
     for t in range(1, halves):
         send_got(t)
         send_right(t)
@@ -245,27 +270,31 @@
 
     locals_[2].wait()
     locals_[3].wait()
-    all_rows = share * n
-    left_blocks = all_rows // BLOCK
     returns = []
     outs = []
+    for copy in lefts:
+        copy.wait_recv()
+    own_left.wait()
+    sibling.start()
     for t in range(halves):
         for copy in rights[t][1:]:
             copy.wait_recv()
-        rights[t][0].wait()
-        if t == 0:
-            for copy in lefts[1:]:
-                copy.wait_recv()
-            lefts[0].wait()
-        for k in range(1, n):
-            gots[t][k].wait_recv()
-        locals_[4 + t].wait()
+        own_rights[t].wait()
         rt = right[t].reshape(BLOCK, BLOCK)
         flipped = rt.astype(jnp.float32).T.astype(jnp.bfloat16)
         cut = slice(t * BLOCK, (t + 1) * BLOCK)
-        for b in range(left_blocks):
-            cols_b = slice(b * BLOCK, (b + 1) * BLOCK)
-            lb = left[b * block_groups:(b + 1) * block_groups].reshape(BLOCK, BLOCK)
+        if t == 0:
+            sibling.wait_recv()
+        for i in reversed(range(left_blocks)):
+            b = peer(i * per) // per
+            cols_b = pl.ds(pl.multiple_of(b * BLOCK, BLOCK), BLOCK)
+            near = range(i * per, (i + 1) * per)
+            for m in near:
+                if m:
+                    gots[t][m].wait_recv()
+                else:
+                    locals_[4 + t].wait()
+            lb = left[pl.ds(b * block_groups, block_groups)].reshape(BLOCK, BLOCK)
             turned = mm(flipped, got[t, cols_b, :], NT)
             rotated = sum(mm(piece, lb, NN) for piece in pieces_of(turned)) * clip
             first_sum = BETA_ONE * m1[cut, cols_b].astype(jnp.float32) + (1.0 - BETA_ONE) * rotated
@@ -277,28 +306,28 @@
             back = sum(mm(rt, piece, NN) for piece in pieces_of(direction))
             result = sum(mm(lb, piece, NT) for piece in pieces_of(back))
             upd[t, cols_b, :] = result.astype(jnp.bfloat16)
-        for k in range(n):
-            src = upd.at[t, share_rows(peer(k))]
-            dst = out_u.at[0, :, out_cols(me, t)]
-            if k == 0:
-                copy = pltpu.make_async_copy(src, dst, ret_r.at[t, 0])
-                outs.append(copy)
-            else:
-                copy = remote(src, dst, ret_s.at[t, k], ret_r.at[t, k], k)
-                returns.append(copy)
-            copy.start()
+            for m in reversed(near):
+                src = upd.at[t, share_rows(peer(m))]
+                dst = out_u.at[0, :, out_cols(me, t)]
+                if m == 0:
+                    copy = pltpu.make_async_copy(src, dst, ret_r.at[t, 0])
+                    outs.append(copy)
+                else:
+                    copy = remote(src, dst, ret_s.at[t, m], ret_r.at[t, m], peer(m))
+                    returns.append(copy)
+                copy.start()
         for index, (value, target) in enumerate(((n1, out_1), (n2, out_2))):
             copy = pltpu.make_async_copy(
                 value.at[cut], target.at[0, cut], loc.at[4 + halves + 2 * t + index])
             copy.start()
             outs.append(copy)
 
-    for copy in hops + zs + fs + lefts[1:]:
+    for copy in hops + zs + fs + lefts + [sibling]:
         copy.wait_send()
     for t in range(halves):
-        for k in range(1, n):
-            gots[t][k].wait_send()
-            rights[t][k].wait_send()
+        for m in range(1, n):
+            gots[t][m].wait_send()
+            rights[t][m].wait_send()
     for copy in outs:
         copy.wait()
     for copy in returns:
@@ -310,8 +339,13 @@
 
 
 def copy_kernel(a, b, c, x, y, z, sems):
-    copies = [pltpu.make_async_copy(src, dst, sems.at[i])
-              for i, (src, dst) in enumerate(((a, x), (b, y), (c, z)))]
+    copies = []
+    for src, dst in ((a, x), (b, y), (c, z)):
+        rows = src.shape[1] // PARTS
+        for i in range(PARTS):
+            cut = pl.ds(i * rows, rows)
+            copies.append(pltpu.make_async_copy(
+                src.at[0, cut], dst.at[0, cut], sems.at[len(copies)]))
     for copy in copies:
         copy.start()
     for copy in copies:
@@ -324,13 +358,13 @@
         out_shape=tuple(jax.ShapeDtypeStruct(a.shape, a.dtype) for a in arrays),
         in_specs=[pl.BlockSpec(memory_space=pltpu.VMEM)] * 3,
         out_specs=(pl.BlockSpec(memory_space=pl.ANY),) * 3,
-        scratch_shapes=[pltpu.SemaphoreType.DMA((3,))],
+        scratch_shapes=[pltpu.SemaphoreType.DMA((3 * PARTS,))],
         compiler_params=pltpu.CompilerParams(vmem_limit_bytes=8 << 20),
     )(*arrays)
 
 
 def fits(gradient, first_moment, basis_store, n):
-    if n % 2:
+    if n < 2 or n & (n - 1):
         return False
     span = n // 2 * SLAB
     width = gradient.shape[2] // n
@@ -340,6 +374,7 @@
         and basis_store.shape[1] % span == 0
         and width % BLOCK == 0
         and all_rows % BLOCK == 0
+        and n % (all_rows // BLOCK) == 0
         and gradient.shape[1] % SLAB == 0
         and all_rows <= 1024
         and width <= 1024

time: 34 us -> 32.2 us (0.947)
  Pallas kernels: 31.9 us -> 30.1 us
    pallas_call x1, Pallas kernels: 30.7 us -> 28.9 us  [local(): pl.pallas_call(functools.partial(kernel, n, groups), out_shape=(jax.Shape...]
where the time goes in v3:
time: 32.2 us; the launch traced here: 32 us
  Pallas kernels  30.1 us (93%)
  between operations  1.93 us (6%)
    pallas_call x1, Pallas kernels, local(): pl.pallas_call(functools.partial(kernel, n, groups), out_shape=(jax.Shape...  28.9 us
    pallas_call x1, Pallas kernels, place(): pl.pallas_call(copy_kernel, out_shape=tuple((jax.ShapeDtypeStruct(a.shape...  1.17 us

profile of v3, /device:TPU:0, one launch (start us, length us, event | category | flops | bytes accessed | tf_op | source)
XLA Modules:
  0.0 32.0 jit_solution(1892292380581437111)
XLA Ops:
  1.9 28.9 %shard_map.85 = (bf16[1,64,4096]{2,1,0:T(8,128)(2,1)S(1)}, bf16[1,512,512]{2,1,0:T(8,128)(2,1)S(1)}, bf16[1,512,512]{2,1,0:T(8,128)(2,1)S(1)}) custom-call(bf16[1,64,4096]{2,1,0:T(8,128)(2,1)} %grad.1, bf16[1,512,512]{2,1,0:T(8,128)(2,1)} %first.1, bf16[1,512,512]{2,1,0:T(8,128)(2,1)} %second.1, bf16[9,4,16,256]{3,2,1,0:T(8,128)(2,1)} %bitcast.1, ...), custom_call_target="tpu_custom_call" | custom-call | tf_op jit(solution)/shard_map/pallas_call | solution.py:404
  30.8 1.2 %shard_map.86 = (bf16[1,64,4096]{2,1,0:T(8,128)(2,1)}, bf16[1,512,512]{2,1,0:T(8,128)(2,1)}, bf16[1,512,512]{2,1,0:T(8,128)(2,1)}) custom-call(bf16[1,64,4096]{2,1,0:T(8,128)(2,1)S(1)} %get-tuple-element.6.a, bf16[1,512,512]{2,1,0:T(8,128)(2,1)S(1)} %get-tuple-element.7.b, bf16[1,512,512]{2,1,0:T(8,128)(2,1)S(1)} %get-tuple-element.8.c), custom_call_target="tpu_custom_call" | custom-call | tf_op jit(solution)/shard_map/pallas_call | solution.py:356

commit v4 on v3

--- a/solution.py
+++ b/solution.py
@@ -177,7 +177,7 @@
         return remote(basis.at[:, d // 2, :, lanes_of(d)], hop.at[me], hop_s.at[m], hop_r.at[m], d)
 
     def got_copy(t, m, d):
-        return remote(grad.at[0, :, out_cols(d, t)], got.at[t, share_rows(me)],
+        return remote(own.at[:, out_cols(d, t)], got.at[t, share_rows(me)],
                       got_s.at[t, m], got_r.at[t, m], d)
 
     def right_copy(t, m, d):
@@ -246,17 +246,16 @@
     for copy in own_rights:
         copy.start()
     lefts_order = [m for m in order if m[0] % 2 == 0]
-    for m, _ in lefts_order:
-        left_copy(m, peer(m)).start()
-
     def send_right(t):
         for pair in order:
             right_copy(t, *pick(pair)).start()
 
     send_right(0)
+    for m, _ in lefts_order:
+        left_copy(m, peer(m)).start()
     for t in range(1, halves):
+        send_right(t)
         send_got(t)
-        send_right(t)
 
     squares = sq_mid[...]
     for k, copy in enumerate(fs):

time: 32.2 us -> 31.9 us (level)
    pallas_call x1, Pallas kernels: 28.9 us -> 28.6 us  [local(): pl.pallas_call(functools.partial(kernel, n, groups), out_shape=(jax.Shape...]
where the time goes in v4:
time: 31.9 us; the launch traced here: 31.7 us
  Pallas kernels  29.8 us (93%)
  between operations  1.93 us (6%)
    pallas_call x1, Pallas kernels, local(): pl.pallas_call(functools.partial(kernel, n, groups), out_shape=(jax.Shape...  28.6 us
    pallas_call x1, Pallas kernels, place(): pl.pallas_call(copy_kernel, out_shape=tuple((jax.ShapeDtypeStruct(a.shape...  1.17 us

profile of v4, /device:TPU:0, one launch (start us, length us, event | category | flops | bytes accessed | tf_op | source)
XLA Modules:
  0.0 31.7 jit_solution(2144340458190521954)
XLA Ops:
  1.9 28.6 %shard_map.85 = (bf16[1,64,4096]{2,1,0:T(8,128)(2,1)S(1)}, bf16[1,512,512]{2,1,0:T(8,128)(2,1)S(1)}, bf16[1,512,512]{2,1,0:T(8,128)(2,1)S(1)}) custom-call(bf16[1,64,4096]{2,1,0:T(8,128)(2,1)} %grad.1, bf16[1,512,512]{2,1,0:T(8,128)(2,1)} %first.1, bf16[1,512,512]{2,1,0:T(8,128)(2,1)} %second.1, bf16[9,4,16,256]{3,2,1,0:T(8,128)(2,1)} %bitcast.1, ...), custom_call_target="tpu_custom_call" | custom-call | tf_op jit(solution)/shard_map/pallas_call | solution.py:403
  30.5 1.2 %shard_map.86 = (bf16[1,64,4096]{2,1,0:T(8,128)(2,1)}, bf16[1,512,512]{2,1,0:T(8,128)(2,1)}, bf16[1,512,512]{2,1,0:T(8,128)(2,1)}) custom-call(bf16[1,64,4096]{2,1,0:T(8,128)(2,1)S(1)} %get-tuple-element.6.a, bf16[1,512,512]{2,1,0:T(8,128)(2,1)S(1)} %get-tuple-element.7.b, bf16[1,512,512]{2,1,0:T(8,128)(2,1)S(1)} %get-tuple-element.8.c), custom_call_target="tpu_custom_call" | custom-call | tf_op jit(solution)/shard_map/pallas_call | solution.py:355
